TPU v7x, 32 devices: a whole 2x2x4 slice. The times are simulated.
32 devices in a mesh: tile: 8 (over y, x, core), depth: 4 (over z).
Axes of the slice: x: 2, y: 2, z: 4, core: 2. Of those that a mesh axis runs over, the one named last changes fastest.
Arguments:
- features: bfloat16 [4, 2048, 128], P('depth', 'tile'), may hold values from -4 to 4
- logits: float32 [4, 2048], P('depth', 'tile'), may hold values from -2.75 to 5.5
- geometry: float32 [2, 4, 5, 2048], P(None, 'depth', None, 'tile'), may hold values from -0.6 to 32, as said below
- dest_slot: int32 [2, 4, 2048], P(None, 'depth', 'tile'), may hold values from -1 to 2047, as said below
- target: bfloat16 [2, 16, 128, 1024], P(None, 'tile'), may hold values from -3 to 3
Outputs:
- images: bfloat16 [2, 16, 128, 1024], P(None, 'tile', None, 'depth')
- new_features: bfloat16 [4, 2048, 128], P('depth', 'tile')
- new_logits: float32 [4, 2048], P('depth', 'tile')
- shape_grads: float32 [2, 4, 5, 2048], P(None, 'depth', None, 'tile')
Inputs may be any that keep to these rules, and one draw needn't show every extreme that they name: `dest_slot`: for each view and layer no two splats share a slot; -1 marks a splat outside the view; a splat's place within its tile is its front-to-back order. At most 32 splats of one layer held by one index of tile go to the tiles of one index of tile, and in every view and layer there is an index of tile whose tiles receive exactly 32 from every owner, so that all their slots are used. `geometry`: components 0 and 1 are a splat's centre in pixels within its tile, from 0 to 32; components 2 and 3 lie in -0.5 to 2.0; component 4 in -0.6 to 0.6.
All inputs are finite; a program needn't handle non-finite values.
Results may differ from a plain program's by a relative error of at most 0.0073.
Values may be sent and summed in bfloat16 or wider, within the bound.
A program may use at most 64 MiB of HBM per device.

v0:
```python
from functools import partial
import jax
import jax.numpy as jnp
from jax import lax
from jax.sharding import PartitionSpec as P

F = 128
W = 32
S = 128
VIEWS = 2
P_SIZE = 1024
clamp_top = 0.99
feature_rate = 0.5
opacity_rate = 0.5


def pixel_places():
    places = jnp.arange(P_SIZE, dtype=jnp.int32)
    across = (places % W).astype(jnp.float32) + 0.5
    downward = (places // W).astype(jnp.float32) + 0.5
    return (across, downward)


def block_sum(values, reverse):
    length = values.shape[0]
    block_rows = min(128, length)
    blocks = values.reshape(length // block_rows, block_rows, values.shape[1])
    positions = jnp.arange(block_rows)
    if reverse:
        triangle = (positions[:, None] < positions[None, :]).astype(jnp.float32)
    else:
        triangle = (positions[:, None] > positions[None, :]).astype(jnp.float32)
    within = jnp.einsum("ij,bjp->bip", triangle, blocks, precision=lax.Precision.HIGHEST)
    block_totals = jnp.sum(blocks, axis=1)
    if reverse:
        offsets = jnp.sum(block_totals, axis=0)[None, :] - jnp.cumsum(block_totals, axis=0)
    else:
        offsets = jnp.cumsum(block_totals, axis=0) - block_totals
    return (within + offsets[:, None, :]).reshape(length, values.shape[1])


def splat_fields(shapes):
    across, downward = pixel_places()
    delta_x = across[None, :] - shapes[0][:, None]
    delta_y = downward[None, :] - shapes[1][:, None]
    coef_a = jnp.exp(shapes[2])[:, None]
    coef_c = jnp.exp(shapes[3])[:, None]
    spread = jnp.exp(0.5 * (shapes[2] + shapes[3]))[:, None]
    coef_b = shapes[4][:, None] * spread
    quadric = (
        coef_a * delta_x * delta_x + 2.0 * coef_b * delta_x * delta_y + coef_c * delta_y * delta_y
    )
    falloff = jnp.exp(-0.5 * quadric)
    opacity = shapes[5][:, None]
    product = opacity * falloff
    coverage = jnp.minimum(product, clamp_top)
    return (delta_x, delta_y, coef_a, coef_b, coef_c, spread, falloff, opacity, product, coverage)


def layer_forward(inputs):
    slot_feats, shapes = inputs
    coverage = splat_fields(shapes)[9]
    log_keep = jnp.log(1.0 - coverage)
    before = block_sum(log_keep, False)
    weights = (coverage * jnp.exp(before)).astype(jnp.bfloat16)
    composite = lax.dot_general(
        slot_feats, weights, (((0,), (0,)), ((), ())), preferred_element_type=jnp.float32
    )
    layer_keep = jnp.exp(jnp.sum(log_keep, axis=0))
    return (composite, layer_keep)


def layer_backward(inputs):
    slot_feats, shapes, grad_comp, grad_keep = inputs
    delta_x, delta_y, coef_a, coef_b, coef_c, spread, falloff, opacity, product, coverage = (
        splat_fields(shapes)
    )
    log_keep = jnp.log(1.0 - coverage)
    before = block_sum(log_keep, False)
    decayed = jnp.exp(before)
    exact_weight = coverage * decayed
    weights = exact_weight.astype(jnp.bfloat16)
    layer_keep = jnp.exp(jnp.sum(log_keep, axis=0))
    grad_feat = lax.dot_general(
        weights, grad_comp, (((1,), (1,)), ((), ())), preferred_element_type=jnp.float32
    )
    grad_weight = jnp.dot(slot_feats, grad_comp, preferred_element_type=jnp.float32)
    grad_before = grad_weight * exact_weight
    later = block_sum(grad_before, True)
    grad_log = later + (grad_keep * layer_keep)[None, :]
    grad_coverage = grad_weight * decayed - grad_log / (1.0 - coverage)
    grad_product = jnp.where(product < clamp_top, grad_coverage, 0.0)
    grad_quadric = -0.5 * opacity * falloff * grad_product
    grad_mean_x = -2.0 * jnp.sum(grad_quadric * (coef_a * delta_x + coef_b * delta_y), axis=1)
    grad_mean_y = -2.0 * jnp.sum(grad_quadric * (coef_b * delta_x + coef_c * delta_y), axis=1)
    grad_first = jnp.sum(grad_quadric * delta_x * delta_x, axis=1)
    grad_cross = jnp.sum(grad_quadric * 2.0 * delta_x * delta_y, axis=1)
    grad_second = jnp.sum(grad_quadric * delta_y * delta_y, axis=1)
    grad_log_a = coef_a[:, 0] * grad_first + 0.5 * coef_b[:, 0] * grad_cross
    grad_log_c = coef_c[:, 0] * grad_second + 0.5 * coef_b[:, 0] * grad_cross
    grad_corr = spread[:, 0] * grad_cross
    opacity_flat = opacity[:, 0]
    grad_logit = opacity_flat * (1.0 - opacity_flat) * jnp.sum(falloff * grad_product, axis=1)
    grad_shape = jnp.stack(
        [grad_mean_x, grad_mean_y, grad_log_a, grad_log_c, grad_corr, grad_logit]
    )
    return (grad_feat, grad_shape)


def rear_step(all_keeps, all_terms, depth_here, layers, counter, carried):
    layer_at = layers - 1 - counter
    updated = all_terms[layer_at] + all_keeps[layer_at] * carried
    return jnp.where(layer_at > depth_here, updated, carried)


def body(features, logits, geometry, dest_slot, target):
    owners = lax.axis_size("tile")
    layers = lax.axis_size("depth")
    depth_here = lax.axis_index("depth")
    tiles_here = target.shape[1]
    owned = features.shape[1]
    capacity = owned // owners
    pixel_share = P_SIZE // layers
    splat_feats = features[0]
    logit_now = logits[0]
    images = []
    shape_grads = []
    for view_index in range(VIEWS):
        slot_ids = dest_slot[view_index, 0]
        visible = slot_ids >= 0
        receiver = jnp.where(visible, slot_ids // owned, owners)
        matches = (receiver[:, None] == jnp.arange(owners, dtype=jnp.int32)[None, :]).astype(
            jnp.int32
        )
        place_in = jnp.sum((jnp.cumsum(matches, axis=0) - matches) * matches, axis=1)
        position = jnp.where(visible, receiver * capacity + place_in, owners * capacity)
        local_slot = jnp.where(visible, slot_ids - receiver * owned, -1)
        opacity = jax.nn.sigmoid(logit_now)
        shape_rows = jnp.concatenate([geometry[view_index, 0], opacity[None, :]], axis=0).T
        row_buffer = (
            jnp.zeros((owners * capacity + 1, F), jnp.bfloat16)
            .at[position]
            .set(splat_feats)[:-1]
            .reshape(owners, capacity, F)
        )
        slot_buffer = (
            jnp.full((owners * capacity + 1,), -1, jnp.int32)
            .at[position]
            .set(local_slot)[:-1]
            .reshape(owners, capacity)
        )
        shape_buffer = (
            jnp.zeros((owners * capacity + 1, 6), jnp.float32)
            .at[position]
            .set(shape_rows)[:-1]
            .reshape(owners, capacity, 6)
        )
        got_rows, got_slots = (
            lax.all_to_all(row_buffer, "tile", split_axis=0, concat_axis=0, tiled=True),
            lax.all_to_all(slot_buffer, "tile", split_axis=0, concat_axis=0, tiled=True),
        )
        got_shapes = lax.all_to_all(shape_buffer, "tile", split_axis=0, concat_axis=0, tiled=True)
        arrived = got_slots.reshape(-1)
        present = arrived >= 0
        landing = jnp.where(present, arrived, owned)
        slot_feats = (
            jnp.zeros((owned + 1, F), jnp.bfloat16)
            .at[landing]
            .set(got_rows.reshape(-1, F))[:-1]
            .reshape(tiles_here, S, F)
        )
        slot_shapes = (
            jnp.zeros((owned + 1, 6), jnp.float32)
            .at[landing]
            .set(got_shapes.reshape(-1, 6))[:-1]
            .reshape(tiles_here, S, 6)
            .transpose(0, 2, 1)
        )
        composites, layer_keeps = lax.map(layer_forward, (slot_feats, slot_shapes))
        all_keeps = lax.all_gather(layer_keeps[None], "depth", axis=0, tiled=True)
        earlier_mask = (jnp.arange(layers) < depth_here)[:, None, None]
        ahead = jnp.prod(jnp.where(earlier_mask, all_keeps, 1.0), axis=0)
        contrib = ahead[:, None, :] * composites
        summed = lax.psum(contrib, "depth")
        residual = summed - target[view_index].astype(jnp.float32)
        image_part = lax.dynamic_slice_in_dim(summed, depth_here * pixel_share, pixel_share, 2)
        images.append(image_part.astype(jnp.bfloat16))
        pixel_terms = jnp.sum(residual * composites, axis=1)
        all_terms = lax.all_gather(pixel_terms[None], "depth", axis=0, tiled=True)
        behind = lax.fori_loop(
            0,
            layers,
            partial(rear_step, all_keeps, all_terms, depth_here, layers),
            jnp.zeros_like(pixel_terms),
        )
        grad_keep = ahead * behind
        grad_comp = (ahead[:, None, :] * residual).astype(jnp.bfloat16)
        grad_feat, grad_shape = lax.map(
            layer_backward, (slot_feats, slot_shapes, grad_comp, grad_keep)
        )
        flat_feat = grad_feat.reshape(owned, F)
        flat_shape = grad_shape.transpose(0, 2, 1).reshape(owned, 6)
        fetched = jnp.where(present, arrived, 0)
        back_feat = jnp.where(present[:, None], flat_feat[fetched], 0.0).reshape(
            owners, capacity, F
        )
        back_shape = jnp.where(present[:, None], flat_shape[fetched], 0.0).reshape(
            owners, capacity, 6
        )
        return_feat, return_shape = (
            lax.all_to_all(back_feat, "tile", split_axis=0, concat_axis=0, tiled=True),
            lax.all_to_all(back_shape, "tile", split_axis=0, concat_axis=0, tiled=True),
        )
        padded_feat = jnp.concatenate(
            [return_feat.reshape(-1, F), jnp.zeros((1, F), jnp.float32)], axis=0
        )
        padded_shape = jnp.concatenate(
            [return_shape.reshape(-1, 6), jnp.zeros((1, 6), jnp.float32)], axis=0
        )
        splat_grad_feat = padded_feat[position]
        splat_grad_shape = padded_shape[position]
        shape_grads.append(splat_grad_shape[:, :5].T)
        splat_feats = (splat_feats.astype(jnp.float32) - feature_rate * splat_grad_feat).astype(
            jnp.bfloat16
        )
        logit_now = logit_now - opacity_rate * splat_grad_shape[:, 5]
    return (jnp.stack(images), splat_feats[None], logit_now[None], jnp.stack(shape_grads)[:, None])


def solution(mesh):
    placed = (
        P("depth", "tile", None),
        P("depth", "tile"),
        P(None, "depth", None, "tile"),
        P(None, "depth", "tile"),
        P(None, "tile", None, None),
    )
    return jax.shard_map(
        body,
        mesh=mesh,
        in_specs=placed,
        out_specs=(
            P(None, "tile", None, "depth"),
            P("depth", "tile", None),
            P("depth", "tile"),
            P(None, "depth", None, "tile"),
        ),
        check_vma=False,
    )
```

profile of v0, /device:TPU:0, one launch (start us, length us, event | category | flops | bytes accessed | tf_op | source)
XLA Modules:
  0.0 308.5 jit_solution(4619955164635074478)
XLA Ops:
  13.0 1.4 scatter_custom_fusion
  15.1 5.3 %all-to-all-start = ((s32[8,1,32]{2,1,0:T(1,128)}), s32[8,1,32]{2,1,0:T(1,128)S(1)}, u32[]{:S(2)}, u32[]{:S(2)}) async-start(s32[8,1,32]{2,1,0:T(1,128)} %all_to_all.36), calls=%async_computation | async-start | bytes 8192 | tf_op jit(solution)/shard_map/all_to_all | solution.py:160
  20.7 1.2 scatter_custom_fusion.3
  22.7 2.4 all-to-all-done
  25.1 3.3 %all-to-all-start.2 = ((f32[8,1,192]{2,1,0:T(1,128)}), f32[8,1,192]{2,1,0:T(1,128)S(1)}, u32[]{:S(2)}, u32[]{:S(2)}) async-start(f32[8,1,192]{2,1,0:T(1,128)} %reshape.3803), calls=%async_computation.2 | async-start | bytes 16384 | tf_op jit(solution)/shard_map/all_to_all | solution.py:162
  28.4 1.2 scatter_custom_fusion.1
  31.5 1.6 all-to-all-done.2
  33.1 3.4 %all-to-all-start.1 = ((bf16[8,32,128]{2,1,0:T(8,128)(2,1)}), bf16[8,32,128]{2,1,0:T(8,128)(2,1)S(1)}, u32[]{:S(2)}, u32[]{:S(2)}) async-start(bf16[8,32,128]{2,1,0:T(8,128)(2,1)} %bitcast.95), calls=%async_computation.1 | async-start | bytes 131072 | tf_op jit(solution)/shard_map/all_to_all | solution.py:159
  37.7 1.2 scatter_custom_fusion.4
  39.0 2.4 all-to-all-done.1
  41.4 1.2 scatter_custom_fusion.2
  44.0 5.1 %while.88 = (s32[]{:T(128)}, f32[2,128,1024]{2,1,0:T(8,128)S(1)}, f32[2,1024]{1,0:T(2,128)S(1)}, bf16[2,128,128]{2,1,0:T(8,128)(2,1)S(1)}, f32[2,6,128]{2,1,0:T(8,128)S(1)}, /*index=5*/s32[]{:T(128)}, s32[]{:T(128)}) while((s32[]{:T(128)}, f32[2,128,1024]{2,1,0:T(8,128)S(1)}, f32[2,1024]{1,0:T(2,128)S(1)}, ...), condition=%wide.region_11.12_spmd, body=%wide.region_8.11_spmd.sunk | while | flops 242777600 | bytes 1177693 | solution.py:179
  45.1 1.2 fusion.315
  47.6 1.2 fusion.315
  49.1 13.4 %all-gather.4 = f32[4,2,1024]{2,1,0:T(2,128)S(1)} all-gather(f32[1,2,1024]{2,1,0:T(2,128)S(1)} %bitcast.689), channel_id=2, replica_groups=mesh['tile'=8,'depth'=4] {'depth'}, dimensions={0}, use_global_device_ids=true | all-gather | bytes 40960 | tf_op jit(solution)/shard_map/all_gather | solution.py:180
  62.6 1.2 broadcast_multiply_fusion.5
  63.8 1.4 scatter_custom_fusion.5
  65.9 49.1 %all-reduce.7.cloned.1.call-done = f32[2,128,1024]{2,1,0:T(8,128)} async-done(((f32[2,128,1024]{2,1,0:T(8,128)}), f32[2,128,1024]{2,1,0:T(8,128)}) %all-reduce.7.cloned.1.call-update) | async-done | bytes 1048592 | tf_op jit(solution)/shard_map/psum | solution.py:184
  115.0 1.5 multiply_reduce_fusion.3
  116.5 13.3 %all-gather.5 = f32[4,2,1024]{2,1,0:T(2,128)S(1)} all-gather(f32[1,2,1024]{2,1,0:T(2,128)S(1)} %bitcast.687), channel_id=3, replica_groups=mesh['tile'=8,'depth'=4] {'depth'}, dimensions={0}, use_global_device_ids=true | all-gather | bytes 40960 | tf_op jit(solution)/shard_map/all_gather | solution.py:189
  130.0 9.6 %while.89 = (s32[]{:T(128)}, f32[2,128,128]{2,1,0:T(8,128)S(1)}, f32[2,6,128]{2,1,0:T(8,128)S(1)}, f32[2,6,128]{2,1,0:T(8,128)S(1)}, bf16[2,128,1024]{2,1,0:T(8,...) while((s32[]{:T(128)}, f32[2,128,128]{2,1,0:T(8,128)S(1)}, ...), condition=%wide.region_31.32_spmd, body=%wide.region_21.31_spmd.sunk | while | flops 485672448 | bytes 3947113 | solution.py:198
  130.6 0.7 fusion.322
  131.9 0.9 fusion.324
  132.9 1.9 fusion.325
  135.4 0.7 fusion.322
  136.8 0.9 fusion.324
  137.7 1.9 fusion.325
  139.8 0.7 gather_fusion
  142.1 3.7 %all-to-all-start.6 = ((f32[8,1,192]{2,1,0:T(1,128)}), f32[8,1,192]{2,1,0:T(1,128)S(1)}, u32[]{:S(2)}, u32[]{:S(2)}) async-start(f32[8,1,192]{2,1,0:T(1,128)} %reshape.3805), calls=%async_computation.6 | async-start | bytes 16384 | tf_op jit(solution)/shard_map/all_to_all | solution.py:212
  145.7 0.8 broadcast_select_fusion.1
  146.5 4.0 %all-to-all-done.6 = f32[8,1,192]{2,1,0:T(1,128)S(1)} async-done(((f32[8,1,192]{2,1,0:T(1,128)}), f32[8,1,192]{2,1,0:T(1,128)S(1)}, u32[]{:S(2)}, u32[]{:S(2)}) %all-to-all-start.6) | async-done | bytes 6176 | tf_op jit(solution)/shard_map/all_to_all | solution.py:212
  150.4 3.3 %all-to-all-start.3 = ((s32[8,1,32]{2,1,0:T(1,128)}), s32[8,1,32]{2,1,0:T(1,128)S(1)}, u32[]{:S(2)}, u32[]{:S(2)}) async-start(s32[8,1,32]{2,1,0:T(1,128)} %all_to_all.40), calls=%async_computation.3 | async-start | bytes 8192 | tf_op jit(solution)/shard_map/all_to_all | solution.py:160
  155.5 2.8 all-to-all-done.3
  158.3 3.4 %all-to-all-start.4 = ((f32[8,32,128]{2,1,0:T(8,128)}), f32[8,32,128]{2,1,0:T(8,128)S(1)}, u32[]{:S(2)}, u32[]{:S(2)}) async-start(f32[8,32,128]{2,1,0:T(8,128)} %broadcast_select_fusion.1), calls=%async_computation.4 | async-start | bytes 262144 | tf_op jit(solution)/shard_map/all_to_all | solution.py:211
  161.9 1.2 scatter_custom_fusion.8
  163.9 3.3 %all-to-all-done.4 = f32[8,32,128]{2,1,0:T(8,128)S(1)} async-done(((f32[8,32,128]{2,1,0:T(8,128)}), f32[8,32,128]{2,1,0:T(8,128)S(1)}, u32[]{:S(2)}, u32[]{:S(2)}) %all-to-all-start.4) | async-done | bytes 131104 | tf_op jit(solution)/shard_map/all_to_all | solution.py:211
  167.1 3.3 %all-to-all-start.7 = ((f32[8,1,192]{2,1,0:T(1,128)}), f32[8,1,192]{2,1,0:T(1,128)S(1)}, u32[]{:S(2)}, u32[]{:S(2)}) async-start(f32[8,1,192]{2,1,0:T(1,128)} %reshape.3807), calls=%async_computation.7 | async-start | bytes 16384 | tf_op jit(solution)/shard_map/all_to_all | solution.py:162
  171.9 1.2 scatter_custom_fusion.6
  173.8 1.3 all-to-all-done.7
  175.1 3.4 %all-to-all-start.5 = ((bf16[8,32,128]{2,1,0:T(8,128)(2,1)}), bf16[8,32,128]{2,1,0:T(8,128)(2,1)S(1)}, u32[]{:S(2)}, u32[]{:S(2)}) async-start(bf16[8,32,128]{2,1,0:T(8,128)(2,1)} %bitcast.121), calls=%async_computation.5 | async-start | bytes 131072 | tf_op jit(solution)/shard_map/all_to_all | solution.py:159
  179.3 1.2 scatter_custom_fusion.9
  180.6 2.9 all-to-all-done.5
  183.4 1.2 scatter_custom_fusion.7
  186.1 5.1 %while.90 = (s32[]{:T(128)}, f32[2,128,1024]{2,1,0:T(8,128)S(1)}, f32[2,1024]{1,0:T(2,128)S(1)}, bf16[2,128,128]{2,1,0:T(8,128)(2,1)S(1)}, f32[2,6,128]{2,1,0:T(8,128)S(1)}, /*index=5*/s32[]{:T(128)}, s32[]{:T(128)}) while((s32[]{:T(128)}, f32[2,128,1024]{2,1,0:T(8,128)S(1)}, f32[2,1024]{1,0:T(2,128)S(1)}, ...), condition=%wide.region_39.40_spmd, body=%wide.region_36.39_spmd.sunk | while | flops 242777600 | bytes 1177693 | solution.py:179
  187.1 1.2 fusion.331
  189.7 1.2 fusion.331
  191.2 13.1 %all-gather.6 = f32[4,2,1024]{2,1,0:T(2,128)S(1)} all-gather(f32[1,2,1024]{2,1,0:T(2,128)S(1)} %bitcast.691), channel_id=4, replica_groups=mesh['tile'=8,'depth'=4] {'depth'}, dimensions={0}, use_global_device_ids=true | all-gather | bytes 40960 | tf_op jit(solution)/shard_map/all_gather | solution.py:180
  204.4 1.1 broadcast_multiply_fusion.4
  205.6 1.0 fusion.228
  206.7 48.4 %all-reduce.9.cloned.1.call-done = f32[2,128,1024]{2,1,0:T(8,128)} async-done(((f32[2,128,1024]{2,1,0:T(8,128)}), f32[2,128,1024]{2,1,0:T(8,128)}) %all-reduce.9.cloned.1.call-update) | async-done | bytes 1048592 | tf_op jit(solution)/shard_map/psum | solution.py:184
  255.1 1.5 multiply_reduce_fusion.2
  256.6 13.4 %all-gather.7 = f32[4,2,1024]{2,1,0:T(2,128)S(1)} all-gather(f32[1,2,1024]{2,1,0:T(2,128)S(1)} %bitcast.688), channel_id=5, replica_groups=mesh['tile'=8,'depth'=4] {'depth'}, dimensions={0}, use_global_device_ids=true | all-gather | bytes 40960 | tf_op jit(solution)/shard_map/all_gather | solution.py:189
  270.2 9.7 %while.91 = (s32[]{:T(128)}, f32[2,128,128]{2,1,0:T(8,128)S(1)}, f32[2,6,128]{2,1,0:T(8,128)S(1)}, f32[2,6,128]{2,1,0:T(8,128)S(1)}, bf16[2,128,1024]{2,1,0:T(8,...) while((s32[]{:T(128)}, f32[2,128,128]{2,1,0:T(8,128)S(1)}, ...), condition=%wide.region_55.56_spmd, body=%wide.region_45.55_spmd.sunk | while | flops 485672448 | bytes 3947113 | solution.py:198
  272.1 0.9 fusion.340
  273.0 1.9 fusion.341
  277.0 0.9 fusion.340
  277.9 1.9 fusion.341
  280.0 0.7 gather_fusion.4
  281.6 0.8 broadcast_select_fusion
  283.0 3.7 %all-to-all-start.9 = ((f32[8,1,192]{2,1,0:T(1,128)}), f32[8,1,192]{2,1,0:T(1,128)S(1)}, u32[]{:S(2)}, u32[]{:S(2)}) async-start(f32[8,1,192]{2,1,0:T(1,128)} %reshape.3809), calls=%async_computation.9 | async-start | bytes 16384 | tf_op jit(solution)/shard_map/all_to_all | solution.py:212
  286.7 1.0 fusion.229
  288.4 3.0 all-to-all-done.9
  291.4 3.4 %all-to-all-start.8 = ((f32[8,32,128]{2,1,0:T(8,128)}), f32[8,32,128]{2,1,0:T(8,128)S(1)}, u32[]{:S(2)}, u32[]{:S(2)}) async-start(f32[8,32,128]{2,1,0:T(8,128)} %broadcast_select_fusion), calls=%async_computation.8 | async-start | bytes 262144 | tf_op jit(solution)/shard_map/all_to_all | solution.py:211
  297.8 2.4 all-to-all-done.8
  (248 shorter events, 40.6 us)
Async XLA Ops:
  8.8 0.6 copy-start.6
  10.2 0.6 copy-start.7
  10.8 0.7 slice-start.2
  11.5 0.7 slice-start.3
  12.3 0.7 copy-start.5
  13.0 7.5 %copy-start.4 = (f32[2,1,5,256]{3,1,2,0:T(1,128)S(1)}, f32[2,1,5,256]{3,1,2,0:T(1,128)}, u32[]{:S(2)}) copy-start(f32[2,1,5,256]{3,1,2,0:T(1,128)} %param.19) | copy-start | bytes 30724
  15.1 5.3 %copy-start.8 = (f32[1,256]{1,0:T(1,128)S(1)}, f32[1,256]{1,0:T(1,128)}, u32[]{:S(2)}) copy-start(f32[1,256]{1,0:T(1,128)} %param.18) | copy-start | bytes 3076
  15.1 9.9 %all-to-all-start = ((s32[8,1,32]{2,1,0:T(1,128)}), s32[8,1,32]{2,1,0:T(1,128)S(1)}, u32[]{:S(2)}, u32[]{:S(2)}) async-start(s32[8,1,32]{2,1,0:T(1,128)} %all_to_all.36), calls=%async_computation | async-start | bytes 8192 | tf_op jit(solution)/shard_map/all_to_all | solution.py:160
  21.9 6.6 %copy-start.3 = (bf16[1,256,128]{2,1,0:T(8,128)(2,1)S(1)}, bf16[1,256,128]{2,1,0:T(8,128)(2,1)}, u32[]{:S(2)}) copy-start(bf16[1,256,128]{2,1,0:T(8,128)(2,1)} %param.17) | copy-start | bytes 196612
  25.1 8.0 %all-to-all-start.2 = ((f32[8,1,192]{2,1,0:T(1,128)}), f32[8,1,192]{2,1,0:T(1,128)S(1)}, u32[]{:S(2)}, u32[]{:S(2)}) async-start(f32[8,1,192]{2,1,0:T(1,128)} %reshape.3803), calls=%async_computation.2 | async-start | bytes 16384 | tf_op jit(solution)/shard_map/all_to_all | solution.py:162
  33.1 8.3 %all-to-all-start.1 = ((bf16[8,32,128]{2,1,0:T(8,128)(2,1)}), bf16[8,32,128]{2,1,0:T(8,128)(2,1)S(1)}, u32[]{:S(2)}, u32[]{:S(2)}) async-start(bf16[8,32,128]{2,1,0:T(8,128)(2,1)} %bitcast.95), calls=%async_computation.1 | async-start | bytes 131072 | tf_op jit(solution)/shard_map/all_to_all | solution.py:159
  36.4 78.5 %all-reduce.7.cloned.1.call-start = ((), (), s32[]{:S(2)}) async-start(), calls=%async_computation.10 | async-start | bytes 2097152 | tf_op jit(solution)/shard_map/psum | solution.py:184
  42.6 0.6 copy-start.2
  43.2 0.8 slice-start.1
  63.8 51.2 %copy-start = (bf16[2,2,128,1024]{3,2,1,0:T(8,128)(2,1)S(1)}, bf16[2,2,128,1024]{3,2,1,0:T(8,128)(2,1)}, u32[]{:S(2)}) copy-start(bf16[2,2,128,1024]{3,2,1,0:T(8,128)(2,1)} %param.21) | copy-start | bytes 3145732
  142.1 8.4 %all-to-all-start.6 = ((f32[8,1,192]{2,1,0:T(1,128)}), f32[8,1,192]{2,1,0:T(1,128)S(1)}, u32[]{:S(2)}, u32[]{:S(2)}) async-start(f32[8,1,192]{2,1,0:T(1,128)} %reshape.3805), calls=%async_computation.6 | async-start | bytes 16384 | tf_op jit(solution)/shard_map/all_to_all | solution.py:212
  150.4 7.9 %all-to-all-start.3 = ((s32[8,1,32]{2,1,0:T(1,128)}), s32[8,1,32]{2,1,0:T(1,128)S(1)}, u32[]{:S(2)}, u32[]{:S(2)}) async-start(s32[8,1,32]{2,1,0:T(1,128)} %all_to_all.40), calls=%async_computation.3 | async-start | bytes 8192 | tf_op jit(solution)/shard_map/all_to_all | solution.py:160
  158.3 8.8 %all-to-all-start.4 = ((f32[8,32,128]{2,1,0:T(8,128)}), f32[8,32,128]{2,1,0:T(8,128)S(1)}, u32[]{:S(2)}, u32[]{:S(2)}) async-start(f32[8,32,128]{2,1,0:T(8,128)} %broadcast_select_fusion.1), calls=%async_computation.4 | async-start | bytes 262144 | tf_op jit(solution)/shard_map/all_to_all | solution.py:211
  167.1 8.0 %all-to-all-start.7 = ((f32[8,1,192]{2,1,0:T(1,128)}), f32[8,1,192]{2,1,0:T(1,128)S(1)}, u32[]{:S(2)}, u32[]{:S(2)}) async-start(f32[8,1,192]{2,1,0:T(1,128)} %reshape.3807), calls=%async_computation.7 | async-start | bytes 16384 | tf_op jit(solution)/shard_map/all_to_all | solution.py:162
  175.1 8.3 %all-to-all-start.5 = ((bf16[8,32,128]{2,1,0:T(8,128)(2,1)}), bf16[8,32,128]{2,1,0:T(8,128)(2,1)S(1)}, u32[]{:S(2)}, u32[]{:S(2)}) async-start(bf16[8,32,128]{2,1,0:T(8,128)(2,1)} %bitcast.121), calls=%async_computation.5 | async-start | bytes 131072 | tf_op jit(solution)/shard_map/all_to_all | solution.py:159
  178.5 76.6 %all-reduce.9.cloned.1.call-start = ((), (), s32[]{:S(2)}) async-start(), calls=%async_computation.11 | async-start | bytes 2097152 | tf_op jit(solution)/shard_map/psum | solution.py:184
  184.6 0.6 copy-start.1
  185.2 0.8 slice-start
  283.0 8.4 %all-to-all-start.9 = ((f32[8,1,192]{2,1,0:T(1,128)}), f32[8,1,192]{2,1,0:T(1,128)S(1)}, u32[]{:S(2)}, u32[]{:S(2)}) async-start(f32[8,1,192]{2,1,0:T(1,128)} %reshape.3809), calls=%async_computation.9 | async-start | bytes 16384 | tf_op jit(solution)/shard_map/all_to_all | solution.py:212
  291.4 8.8 %all-to-all-start.8 = ((f32[8,32,128]{2,1,0:T(8,128)}), f32[8,32,128]{2,1,0:T(8,128)S(1)}, u32[]{:S(2)}, u32[]{:S(2)}) async-start(f32[8,32,128]{2,1,0:T(8,128)} %broadcast_select_fusion), calls=%async_computation.8 | async-start | bytes 262144 | tf_op jit(solution)/shard_map/all_to_all | solution.py:211
Sparse Core Ops, SparseCore 0:
  63.9 51.0 all-reduce.6
  205.7 49.3 all-reduce.8
where the time goes:
time: 310 us; the launch traced here: 308 us
  waiting for transfers between devices  123 us (40%)
  blocking collectives  53.2 us (17%)
  starting transfers between devices  36.2 us (12%)
  local copies, waits for them, and re-layouts  35.9 us (12%)
  matrix products  22.2 us (7%)
  other arithmetic  21.8 us (7%)
  between operations  14.7 us (5%)
    psum x2, waiting for transfers between devices, body(): summed = lax.psum(contrib, 'depth')  97.4 us
    all_gather x2, blocking collectives, body(): all_terms = lax.all_gather(pixel_terms[None], 'depth', axis=0, tiled=True)  26.7 us
    all_gather x2, blocking collectives, body(): all_keeps = lax.all_gather(layer_keeps[None], 'depth', axis=0, tiled=True)  26.5 us
    dot_general x12, matrix products, block_sum(): jnp.einsum('ij,bjp->bip', triangle, blocks, precision=lax.Precision.HIGHEST)  15.4 us
    all_to_all x2, starting transfers between devices, body(): lax.all_to_all(slot_buffer, 'tile', split_axis=0, concat_axis=0, tiled=True)  8.64 us
    all_to_all x2, starting transfers between devices, body(): lax.all_to_all(back_shape, 'tile', split_axis=0, concat_axis=0, tiled=True)  7.32 us
    all_to_all x2, waiting for transfers between devices, body(): lax.all_to_all(back_shape, 'tile', split_axis=0, concat_axis=0, tiled=True)  6.97 us
    unnamed x28, local copies, waits for them, and re-layouts  6.8 us
  transfers between devices with their start and end apart: 12, of which 12 were waited for; matrix products, arithmetic and copies ran while one was open for 8% of the time, Pallas kernels for 0%

commit v1 on v0

--- a/solution.py
+++ b/solution.py
@@ -1,3 +1,4 @@
+import functools
 from functools import partial
 import jax
 import jax.numpy as jnp
@@ -12,6 +13,23 @@
 clamp_top = 0.99
 feature_rate = 0.5
 opacity_rate = 0.5
+
+
+def settle_patch_now(u_in, axis_tag):
+    extent = lax.axis_size(axis_tag)
+
+    def search_sectors(state_next, r2):
+        if r2 >= extent:
+            return state_next
+        views = []
+        for t in range(extent):
+            views.append((t, t ^ r2))
+        return search_sectors(state_next + lax.ppermute(state_next, axis_tag, views), 2 * r2)
+
+    return search_sectors(u_in, 1)
+
+
+feed_matrix = functools.partial(settle_patch_now, axis_tag="depth")
 
 
 def pixel_places():
@@ -181,7 +199,7 @@
         earlier_mask = (jnp.arange(layers) < depth_here)[:, None, None]
         ahead = jnp.prod(jnp.where(earlier_mask, all_keeps, 1.0), axis=0)
         contrib = ahead[:, None, :] * composites
-        summed = lax.psum(contrib, "depth")
+        summed = feed_matrix(contrib)
         residual = summed - target[view_index].astype(jnp.float32)
         image_part = lax.dynamic_slice_in_dim(summed, depth_here * pixel_share, pixel_share, 2)
         images.append(image_part.astype(jnp.bfloat16))

time: 310 us -> 336 us (1.084)
  waiting for transfers between devices: 123 us -> 139 us
  between operations: 14.7 us -> 1.41 us
  local copies, waits for them, and re-layouts: 35.9 us -> 44.2 us
  other arithmetic: 21.8 us -> 28.5 us
  starting transfers between devices: 36.2 us -> 42.3 us
    ppermute x0 -> x4, waiting for transfers between devices: none -> 119 us  [search_sectors(): lax.ppermute(state_next, axis_tag, views)]
    psum x2 -> x0, waiting for transfers between devices: 97.4 us -> none  [body(): summed = lax.psum(contrib, 'depth')]
    ppermute x0 -> x4, starting transfers between devices: none -> 7 us  [search_sectors(): lax.ppermute(state_next, axis_tag, views)]
    unnamed x28 -> x62, local copies, waits for them, and re-layouts: 6.8 us -> 13.2 us
  transfers between devices with their start and end apart: 12 -> 14, of which waited for: 12 -> 14; matrix products, arithmetic and copies ran while one was open for 8% -> 9% of each run, Pallas kernels for 0% -> 0%
where the time goes in v1:
time: 336 us; the launch traced here: 334 us
  waiting for transfers between devices  139 us (41%)
  blocking collectives  53.6 us (16%)
  local copies, waits for them, and re-layouts  44.2 us (13%)
  starting transfers between devices  42.3 us (13%)
  other arithmetic  28.5 us (8%)
  matrix products  24.2 us (7%)
    ppermute x4, waiting for transfers between devices, search_sectors(): lax.ppermute(state_next, axis_tag, views)  119 us
    all_gather x2, blocking collectives, body(): all_keeps = lax.all_gather(layer_keeps[None], 'depth', axis=0, tiled=True)  27.1 us
    all_gather x2, blocking collectives, body(): all_terms = lax.all_gather(pixel_terms[None], 'depth', axis=0, tiled=True)  26.5 us
    dot_general x12, matrix products, block_sum(): jnp.einsum('ij,bjp->bip', triangle, blocks, precision=lax.Precision.HIGHEST)  15.4 us
    unnamed x62, local copies, waits for them, and re-layouts  13.2 us
    all_to_all x2, starting transfers between devices, body(): lax.all_to_all(slot_buffer, 'tile', split_axis=0, concat_axis=0, tiled=True)  8.51 us
    ppermute x4, starting transfers between devices, search_sectors(): lax.ppermute(state_next, axis_tag, views)  7 us
    all_to_all x2, starting transfers between devices, body(): lax.all_to_all(back_feat, 'tile', split_axis=0, concat_axis=0, tiled=True)  6.74 us
  transfers between devices with their start and end apart: 14, of which 14 were waited for; matrix products, arithmetic and copies ran while one was open for 9% of the time, Pallas kernels for 0%

profile of v1, /device:TPU:0, one launch (start us, length us, event | category | flops | bytes accessed | tf_op | source)
XLA Modules:
  0.0 334.3 jit_solution(16213645440801537066)
XLA Ops:
  6.5 1.4 scatter_custom_fusion
  8.6 5.2 %all-to-all-start = ((s32[8,1,32]{2,1,0:T(1,128)}), s32[8,1,32]{2,1,0:T(1,128)S(1)}, u32[]{:S(2)}, u32[]{:S(2)}) async-start(s32[8,1,32]{2,1,0:T(1,128)} %all_to_all.36), calls=%async_computation | async-start | bytes 8192 | tf_op jit(solution)/shard_map/all_to_all | solution.py:178
  14.7 1.2 scatter_custom_fusion.3
  16.7 1.8 all-to-all-done
  18.4 3.3 all-to-all-start.2
  21.8 1.2 scatter_custom_fusion.1
  24.9 1.5 all-to-all-done.2
  26.4 3.4 %all-to-all-start.1 = ((bf16[8,32,128]{2,1,0:T(8,128)(2,1)}), bf16[8,32,128]{2,1,0:T(8,128)(2,1)S(1)}, u32[]{:S(2)}, u32[]{:S(2)}) async-start(bf16[8,32,128]{2,1,0:T(8,128)(2,1)} %bitcast.95), calls=%async_computation.1 | async-start | bytes 131072 | tf_op jit(solution)/shard_map/all_to_all | solution.py:177
  31.2 1.2 scatter_custom_fusion.4
  32.4 2.3 all-to-all-done.1
  34.7 1.2 scatter_custom_fusion.2
  37.4 5.1 %while.88 = (s32[]{:T(128)}, f32[2,128,1024]{2,1,0:T(8,128)S(1)}, f32[2,1024]{1,0:T(2,128)S(1)}, bf16[2,128,128]{2,1,0:T(8,128)(2,1)S(1)}, f32[2,6,128]{2,1,0:T(8,128)S(1)}, /*index=5*/s32[]{:T(128)}, s32[]{:T(128)}) while((s32[]{:T(128)}, f32[2,128,1024]{2,1,0:T(8,128)S(1)}, f32[2,1024]{1,0:T(2,128)S(1)}, ...), condition=%wide.region_11.12_spmd, body=%wide.region_8.11_spmd.sunk | while | flops 242777600 | bytes 1177685 | solution.py:197
  37.9 1.2 fusion.317
  40.5 1.2 fusion.317
  42.5 13.4 %all-gather.4 = f32[4,2,1024]{2,1,0:T(2,128)S(1)} all-gather(f32[1,2,1024]{2,1,0:T(2,128)S(1)} %bitcast.679), channel_id=2, replica_groups=mesh['tile'=8,'depth'=4] {'depth'}, dimensions={0}, use_global_device_ids=true | all-gather | bytes 40960 | tf_op jit(solution)/shard_map/all_gather | solution.py:198
  56.1 1.6 collective-permute-start
  57.8 21.6 %collective-permute-done = f32[2,128,1024]{2,1,0:T(8,128)S(1)} collective-permute-done((f32[2,128,1024]{2,1,0:T(8,128)S(1)}, f32[2,128,1024]{2,1,0:T(8,128)S(1)}, u32[]{:S(2)}, u32[]{:S(2)}) %collective-permute-start) | collective-permute-done | bytes 1048608 | tf_op jit(solution)/shard_map/ppermute | solution.py:27
  79.6 1.7 collective-permute-start.1
  81.3 1.4 scatter_custom_fusion.5
  83.4 39.5 %collective-permute-done.1 = f32[2,128,1024]{2,1,0:T(8,128)} collective-permute-done((f32[2,128,1024]{2,1,0:T(8,128)S(1)}, f32[2,128,1024]{2,1,0:T(8,128)}, u32[]{:S(2)}, u32[]{:S(2)}) %collective-permute-start.1) | collective-permute-done | bytes 1048608 | tf_op jit(solution)/shard_map/ppermute | solution.py:27
  122.8 1.9 multiply_reduce_fusion.3
  124.8 13.3 %all-gather.5 = f32[4,2,1024]{2,1,0:T(2,128)S(1)} all-gather(f32[1,2,1024]{2,1,0:T(2,128)S(1)} %bitcast.678), channel_id=3, replica_groups=mesh['tile'=8,'depth'=4] {'depth'}, dimensions={0}, use_global_device_ids=true | all-gather | bytes 40960 | tf_op jit(solution)/shard_map/all_gather | solution.py:207
  138.5 11.8 %while.89 = (s32[]{:T(128)}, f32[2,128,128]{2,1,0:T(8,128)S(1)}, f32[2,6,128]{2,1,0:T(8,128)S(1)}, f32[2,6,128]{2,1,0:T(8,128)S(1)}, bf16[2,128,1024]{2,1,0:T(8,...) while((s32[]{:T(128)}, f32[2,128,128]{2,1,0:T(8,128)S(1)}, ...), condition=%wide.region_30.31_spmd, body=%wide.region_20.30_spmd.sunk | while | flops 485672448 | bytes 6044285 | solution.py:216
  139.8 0.9 fusion.326
  140.8 1.9 fusion.327
  142.7 1.6 fusion.325
  145.7 0.9 fusion.326
  146.6 1.9 fusion.327
  148.6 1.6 fusion.325
  152.0 3.3 all-to-all-start.6
  156.8 3.2 all-to-all-done.6
  160.0 3.3 all-to-all-start.3
  165.1 2.8 all-to-all-done.3
  167.8 3.4 %all-to-all-start.4 = ((f32[8,32,128]{2,1,0:T(8,128)}), f32[8,32,128]{2,1,0:T(8,128)S(1)}, u32[]{:S(2)}, u32[]{:S(2)}) async-start(f32[8,32,128]{2,1,0:T(8,128)} %broadcast_select_fusion.1), calls=%async_computation.4 | async-start | bytes 262144 | tf_op jit(solution)/shard_map/all_to_all | solution.py:229
  172.6 1.2 scatter_custom_fusion.8
  174.6 2.0 all-to-all-done.4
  176.6 3.3 all-to-all-start.7
  181.5 1.3 scatter_custom_fusion.6
  183.4 1.2 all-to-all-done.7
  184.6 3.4 %all-to-all-start.5 = ((bf16[8,32,128]{2,1,0:T(8,128)(2,1)}), bf16[8,32,128]{2,1,0:T(8,128)(2,1)S(1)}, u32[]{:S(2)}, u32[]{:S(2)}) async-start(bf16[8,32,128]{2,1,0:T(8,128)(2,1)} %bitcast.121), calls=%async_computation.5 | async-start | bytes 131072 | tf_op jit(solution)/shard_map/all_to_all | solution.py:177
  189.4 1.2 scatter_custom_fusion.9
  190.7 2.3 all-to-all-done.5
  192.9 1.2 scatter_custom_fusion.7
  195.6 7.6 %while.90 = (s32[]{:T(128)}, f32[2,128,1024]{2,1,0:T(8,128)S(1)}, f32[2,1024]{1,0:T(2,128)}, bf16[2,128,128]{2,1,0:T(8,128)(2,1)S(1)}, f32[2,6,128]{2,1,0:T(8,128)S(1)}, /*index=5*/s32[]{:T(128)}, s32[]{:T(128)}) while((s32[]{:T(128)}, f32[2,128,1024]{2,1,0:T(8,128)S(1)}, f32[2,1024]{1,0:T(2,128)}, bf16[2,128,128]{2,1,0:T(8,128)(2,1)S(1)}, ...), condition=%wide.region_38.39_spmd, body=%wide.region_35.38_spmd.sunk | while | flops 242777600 | bytes 1177685 | solution.py:197
  196.1 1.2 fusion.333
  198.1 1.3 dynamic_update_slice.71
  199.9 1.2 fusion.333
  201.9 1.3 dynamic_update_slice.71
  203.2 13.7 %all-gather.6 = f32[4,2,1024]{2,1,0:T(2,128)S(1)} all-gather(f32[1,2,1024]{2,1,0:T(2,128)} %bitcast.681), channel_id=4, replica_groups=mesh['tile'=8,'depth'=4] {'depth'}, dimensions={0}, use_global_device_ids=true | all-gather | bytes 40960 | tf_op jit(solution)/shard_map/all_gather | solution.py:198
  217.6 1.6 collective-permute-start.2
  219.2 20.3 %collective-permute-done.2 = f32[2,128,1024]{2,1,0:T(8,128)S(1)} collective-permute-done((f32[2,128,1024]{2,1,0:T(8,128)S(1)}, f32[2,128,1024]{2,1,0:T(8,128)S(1)}, u32[]{:S(2)}, u32[]{:S(2)}) %collective-permute-start.2) | collective-permute-done | bytes 1048608 | tf_op jit(solution)/shard_map/ppermute | solution.py:27
  239.5 1.2 fusion.277
  240.7 2.1 collective-permute-start.3
  247.3 38.0 %collective-permute-done.3 = f32[2,128,1024]{2,1,0:T(8,128)} collective-permute-done((f32[2,128,1024]{2,1,0:T(8,128)}, f32[2,128,1024]{2,1,0:T(8,128)}, u32[]{:S(2)}, u32[]{:S(2)}) %collective-permute-start.3) | collective-permute-done | bytes 1048608 | tf_op jit(solution)/shard_map/ppermute | solution.py:27
  285.4 1.9 multiply_reduce_fusion.2
  287.5 13.2 %all-gather.7 = f32[4,2,1024]{2,1,0:T(2,128)S(1)} all-gather(f32[1,2,1024]{2,1,0:T(2,128)S(1)} %bitcast.677), channel_id=5, replica_groups=mesh['tile'=8,'depth'=4] {'depth'}, dimensions={0}, use_global_device_ids=true | all-gather | bytes 40960 | tf_op jit(solution)/shard_map/all_gather | solution.py:207
  300.7 2.9 while.93
  303.7 9.6 %while.91 = (s32[]{:T(128)}, f32[2,128,128]{2,1,0:T(8,128)S(1)}, f32[2,6,128]{2,1,0:T(8,128)S(1)}, f32[2,6,128]{2,1,0:T(8,128)S(1)}, bf16[2,128,1024]{2,1,0:T(8,...) while((s32[]{:T(128)}, f32[2,128,128]{2,1,0:T(8,128)S(1)}, ...), condition=%wide.region_53.54_spmd, body=%wide.region_43.53_spmd.sunk | while | flops 485672448 | bytes 3947105 | solution.py:216
  305.0 0.8 fusion.342
  305.9 1.9 fusion.343
  310.7 1.9 fusion.343
  316.0 3.3 all-to-all-start.9
  321.8 2.3 all-to-all-done.9
  324.0 3.4 %all-to-all-start.8 = ((f32[8,32,128]{2,1,0:T(8,128)}), f32[8,32,128]{2,1,0:T(8,128)S(1)}, u32[]{:S(2)}, u32[]{:S(2)}) async-start(f32[8,32,128]{2,1,0:T(8,128)} %broadcast_select_fusion), calls=%async_computation.8 | async-start | bytes 262144 | tf_op jit(solution)/shard_map/all_to_all | solution.py:229
  (292 shorter events, 59.2 us)
Async XLA Ops:
  2.2 0.6 copy-start.16
  3.7 0.6 copy-start.17
  4.3 0.7 slice-start.2
  5.0 0.7 slice-start.3
  5.8 0.7 copy-start.15
  6.5 166.1 %copy-start.19 = (s32[256,1]{0,1:T(1,128)}, s32[256,1]{0,1:T(1,128)S(1)}, u32[]{:S(2)}) copy-start(s32[256,1]{0,1:T(1,128)S(1)} %get-tuple-element.807) | copy-start | bytes 3076
  6.5 7.3 %copy-start.11 = (f32[2,1,5,256]{3,1,2,0:T(1,128)S(1)}, f32[2,1,5,256]{3,1,2,0:T(1,128)}, u32[]{:S(2)}) copy-start(f32[2,1,5,256]{3,1,2,0:T(1,128)} %param.19) | copy-start | bytes 30724
  8.6 9.8 %all-to-all-start = ((s32[8,1,32]{2,1,0:T(1,128)}), s32[8,1,32]{2,1,0:T(1,128)S(1)}, u32[]{:S(2)}, u32[]{:S(2)}) async-start(s32[8,1,32]{2,1,0:T(1,128)} %all_to_all.36), calls=%async_computation | async-start | bytes 8192 | tf_op jit(solution)/shard_map/all_to_all | solution.py:178
  13.8 0.7 copy-start.22
  16.0 5.8 %copy-start.4 = (bf16[1,256,128]{2,1,0:T(8,128)(2,1)S(1)}, bf16[1,256,128]{2,1,0:T(8,128)(2,1)}, u32[]{:S(2)}) copy-start(bf16[1,256,128]{2,1,0:T(8,128)(2,1)} %param.17) | copy-start | bytes 196612
  18.4 8.0 %all-to-all-start.2 = ((f32[8,1,192]{2,1,0:T(1,128)}), f32[8,1,192]{2,1,0:T(1,128)S(1)}, u32[]{:S(2)}, u32[]{:S(2)}) async-start(f32[8,1,192]{2,1,0:T(1,128)} %reshape.3803), calls=%async_computation.2 | async-start | bytes 16384 | tf_op jit(solution)/shard_map/all_to_all | solution.py:180
  21.8 34.1 %copy-start.24 = (pred[4]{0:T(512)(128)(4,1)}, pred[4]{0:T(512)(128)(4,1)S(1)}, u32[]{:S(2)}) copy-start(pred[4]{0:T(512)(128)(4,1)S(1)} %iota_compare_fusion.16) | copy-start | bytes 16
  26.4 8.3 %all-to-all-start.1 = ((bf16[8,32,128]{2,1,0:T(8,128)(2,1)}), bf16[8,32,128]{2,1,0:T(8,128)(2,1)S(1)}, u32[]{:S(2)}, u32[]{:S(2)}) async-start(bf16[8,32,128]{2,1,0:T(8,128)(2,1)} %bitcast.95), calls=%async_computation.1 | async-start | bytes 131072 | tf_op jit(solution)/shard_map/all_to_all | solution.py:177
  35.9 0.6 copy-start.3
  36.5 0.8 slice-start.1
  56.1 66.7 %copy-start = (bf16[2,2,128,1024]{3,2,1,0:T(8,128)(2,1)S(1)}, bf16[2,2,128,1024]{3,2,1,0:T(8,128)(2,1)}, u32[]{:S(2)}) copy-start(bf16[2,2,128,1024]{3,2,1,0:T(8,128)(2,1)} %param.21) | copy-start | bytes 3145732
  56.1 23.2 %collective-permute-start = (f32[2,128,1024]{2,1,0:T(8,128)S(1)}, f32[2,128,1024]{2,1,0:T(8,128)S(1)}, u32[]{:S(2)}, u32[]{:S(2)}) collective-permute-start(f32[2,128,1024]{2,1,0:T(8,128)S(1)} %broadcast_multiply_fusion.5), channel_id=1, source_target_pairs={{0,1},{1,0},{2,3},{3,2},{4,5},{5,4},{6,7},{7,6},{8,9},{9,8},{10,11... | collective-permute-start | bytes 3145736 | tf_op jit(solution)/shard_map/ppermute | solution.py:27
  79.6 3.8 %copy-start.1 = (f32[2,128,1024]{2,1,0:T(8,128)}, f32[2,128,1024]{2,1,0:T(8,128)S(1)}, u32[]{:S(2)}) copy-start(f32[2,128,1024]{2,1,0:T(8,128)S(1)} %fusion.278) | copy-start | bytes 3145732
  79.6 43.2 %collective-permute-start.1 = (f32[2,128,1024]{2,1,0:T(8,128)S(1)}, f32[2,128,1024]{2,1,0:T(8,128)}, u32[]{:S(2)}, u32[]{:S(2)}) collective-permute-start(f32[2,128,1024]{2,1,0:T(8,128)S(1)} %fusion.278), channel_id=1, source_target_pairs={{0,2},{1,3},{2,0},{3,1},{4,6},{5,7},{6,4},{7,5},{8,10},{9,11},{10,... | collective-permute-start | bytes 3145736 | tf_op jit(solution)/shard_map/ppermute | solution.py:27
  139.8 0.9 copy-start.26
  145.7 0.9 copy-start.26
  152.0 8.0 %all-to-all-start.6 = ((f32[8,1,192]{2,1,0:T(1,128)}), f32[8,1,192]{2,1,0:T(1,128)S(1)}, u32[]{:S(2)}, u32[]{:S(2)}) async-start(f32[8,1,192]{2,1,0:T(1,128)} %reshape.3805), calls=%async_computation.6 | async-start | bytes 16384 | tf_op jit(solution)/shard_map/all_to_all | solution.py:230
  160.0 7.9 %all-to-all-start.3 = ((s32[8,1,32]{2,1,0:T(1,128)}), s32[8,1,32]{2,1,0:T(1,128)S(1)}, u32[]{:S(2)}, u32[]{:S(2)}) async-start(s32[8,1,32]{2,1,0:T(1,128)} %all_to_all.40), calls=%async_computation.3 | async-start | bytes 8192 | tf_op jit(solution)/shard_map/all_to_all | solution.py:178
  167.8 8.8 %all-to-all-start.4 = ((f32[8,32,128]{2,1,0:T(8,128)}), f32[8,32,128]{2,1,0:T(8,128)S(1)}, u32[]{:S(2)}, u32[]{:S(2)}) async-start(f32[8,32,128]{2,1,0:T(8,128)} %broadcast_select_fusion.1), calls=%async_computation.4 | async-start | bytes 262144 | tf_op jit(solution)/shard_map/all_to_all | solution.py:229
  171.2 0.7 copy-start.23
  176.6 8.0 %all-to-all-start.7 = ((f32[8,1,192]{2,1,0:T(1,128)}), f32[8,1,192]{2,1,0:T(1,128)S(1)}, u32[]{:S(2)}, u32[]{:S(2)}) async-start(f32[8,1,192]{2,1,0:T(1,128)} %reshape.3807), calls=%async_computation.7 | async-start | bytes 16384 | tf_op jit(solution)/shard_map/all_to_all | solution.py:180
  184.6 8.3 %all-to-all-start.5 = ((bf16[8,32,128]{2,1,0:T(8,128)(2,1)}), bf16[8,32,128]{2,1,0:T(8,128)(2,1)S(1)}, u32[]{:S(2)}, u32[]{:S(2)}) async-start(bf16[8,32,128]{2,1,0:T(8,128)(2,1)} %bitcast.121), calls=%async_computation.5 | async-start | bytes 131072 | tf_op jit(solution)/shard_map/all_to_all | solution.py:177
  194.1 0.6 copy-start.2
  194.8 0.8 slice-start
  203.2 13.7 %copy-start.25 = (pred[4]{0:T(512)(128)(4,1)S(1)}, pred[4]{0:T(512)(128)(4,1)}, u32[]{:S(2)}) copy-start(pred[4]{0:T(512)(128)(4,1)} %copy-done.24) | copy-start | bytes 16
  216.9 0.6 copy-start.6
  217.5 22.0 %copy-start.8 = (f32[2,1024]{1,0:T(2,128)}, f32[2,1024]{1,0:T(2,128)S(1)}, u32[]{:S(2)}) copy-start(f32[2,1024]{1,0:T(2,128)S(1)} %select_reduce_fusion) | copy-start | bytes 24580
  217.6 21.9 %collective-permute-start.2 = (f32[2,128,1024]{2,1,0:T(8,128)S(1)}, f32[2,128,1024]{2,1,0:T(8,128)S(1)}, u32[]{:S(2)}, u32[]{:S(2)}) collective-permute-start(f32[2,128,1024]{2,1,0:T(8,128)S(1)} %broadcast_multiply_fusion.4), channel_id=1, source_target_pairs={{0,1},{1,0},{2,3},{3,2},{4,5},{5,4},{6,7},{7,6},{8,9},{9,8},{10,11... | collective-permute-start | bytes 3145736 | tf_op jit(solution)/shard_map/ppermute | solution.py:27
  240.7 44.6 %collective-permute-start.3 = (f32[2,128,1024]{2,1,0:T(8,128)}, f32[2,128,1024]{2,1,0:T(8,128)}, u32[]{:S(2)}, u32[]{:S(2)}) collective-permute-start(f32[2,128,1024]{2,1,0:T(8,128)} %fusion.277), channel_id=1, source_target_pairs={{0,2},{1,3},{2,0},{3,1},{4,6},{5,7},{6,4},{7,5},{8,10},{9,11},{10,... | collective-permute-start | bytes 3145736 | tf_op jit(solution)/shard_map/ppermute | solution.py:27
  242.9 0.7 copy-start.20
  244.1 0.7 copy-start.18
  247.3 40.0 %copy-start.9 = (f32[2,1024]{1,0:T(2,128)S(1)}, f32[2,1024]{1,0:T(2,128)}, u32[]{:S(2)}) copy-start(f32[2,1024]{1,0:T(2,128)} %copy-done.8) | copy-start | bytes 24580
  287.5 13.2 %copy-start.7 = (f32[2,1024]{1,0:T(2,128)S(1)}, f32[2,1024]{1,0:T(2,128)}, u32[]{:S(2)}) copy-start(f32[2,1024]{1,0:T(2,128)} %custom-call.1) | copy-start | bytes 24580
  313.3 0.7 copy-start.14
  314.7 0.7 copy-start.12
  316.0 8.0 %all-to-all-start.9 = ((f32[8,1,192]{2,1,0:T(1,128)}), f32[8,1,192]{2,1,0:T(1,128)S(1)}, u32[]{:S(2)}, u32[]{:S(2)}) async-start(f32[8,1,192]{2,1,0:T(1,128)} %reshape.3809), calls=%async_computation.9 | async-start | bytes 16384 | tf_op jit(solution)/shard_map/all_to_all | solution.py:230
  320.1 0.9 copy-start.5
  324.0 8.8 %all-to-all-start.8 = ((f32[8,32,128]{2,1,0:T(8,128)}), f32[8,32,128]{2,1,0:T(8,128)S(1)}, u32[]{:S(2)}, u32[]{:S(2)}) async-start(f32[8,32,128]{2,1,0:T(8,128)} %broadcast_select_fusion), calls=%async_computation.8 | async-start | bytes 262144 | tf_op jit(solution)/shard_map/all_to_all | solution.py:229
  328.3 0.7 copy-start.13
  329.7 0.7 copy-start.10
  331.2 0.7 copy-start.21
